TPU v7x, 32 devices: a whole 2x2x4 slice. The times are simulated.
32 devices in a mesh: seq: 8 (over y, x, core), mp: 4 (over z).
Axes of the slice: x: 2, y: 2, z: 4, core: 2. Of those that a mesh axis runs over, the one named last changes fastest.
Arguments:
- tokens: bfloat16 [64, 2048, 1024], P('mp', 'seq'), may hold values from -6 to 6
- cotangent: bfloat16 [64, 2048, 1024], P('mp', 'seq'), may hold values from -6 to 6
- lengths: int32 [64], P('mp'), may hold values from 256 to 2048, as said below
- routed: int32 [64, 256], P('mp', 'seq'), may hold values from 0 to 2047, as said below
- gain_attn: float32 [1024], replicated, may hold values from 0.5 to 1.5
- gain_mlp: float32 [1024], replicated, may hold values from 0.5 to 1.5
- router: float32 [1024], replicated, may hold values from -0.1875 to 0.1875
- w_qkv: bfloat16 [3, 1024, 1024], P(None, None, 'mp'), may hold values from -0.1875 to 0.1875
- w_out: bfloat16 [1024, 1024], P('mp'), may hold values from -1.5 to 1.5
- w_mlp: bfloat16 [4096, 2, 1024], P('mp'), may hold values from -0.1875 to 0.1875
Outputs:
- layer_out: bfloat16 [64, 2048, 1024], P('mp', 'seq')
- grad_tokens: bfloat16 [64, 2048, 1024], P('mp', 'seq')
- grad_gain_attn: float32 [1024], replicated
- grad_gain_mlp: float32 [1024], replicated
- grad_router: float32 [1024], replicated
- grad_qkv: float32 [3, 1024, 1024], P(None, None, 'mp')
- grad_out: float32 [1024, 1024], P('mp')
- grad_mlp: float32 [4096, 2, 1024], P('mp')
Inputs may be any that keep to these rules, and one draw needn't show every extreme that they name: `lengths`: multiples of 8; of the two sequences 2 i and 2 i + 1 (aligned pairs) at most one is longer than 1024; among the 16 sequences of each index of mp one has length 2048 and its partner in the pair has length 256. `routed`: entry j of a sequence lies in 8 j to 8 j + 7; entries with j at or past lengths / 8 point at padding.
All inputs are finite; a program needn't handle non-finite values.
Results may differ from a plain program's by a relative error of at most 0.017.
Values may be sent and summed in bfloat16 or wider, within the bound.
No kernel may reach another device: no remote copies, remote signals or barrier semaphores. Data moves between devices by JAX's collectives and lax.ppermute only.
A program may use at most 192 MiB of HBM per device.

v0:
```python
import jax
import jax.numpy as jnp
from jax import lax
from jax.sharding import PartitionSpec as P

HEAD = 64
EPSILON = 1e-06
NEGATIVE = -1e30
BEST = lax.Precision.HIGHEST
CONTRACT_ROWS = (((0,), (0,)), ((), ()))
CONTRACT_COLS = (((1,), (1,)), ((), ()))


def rms_scale(values):
    return lax.rsqrt(jnp.mean(values * values, axis=-1, keepdims=True) + EPSILON)


def norm_back(grad_normed, unit_rows, scale, gain):
    scaled = gain * grad_normed
    return scale * (scaled - unit_rows * jnp.mean(unit_rows * scaled, axis=-1, keepdims=True))


def gelu_tanh(values):
    return jax.nn.gelu(values, approximate=True)


def split_heads(heads_in, unit_rows):
    local_width = heads_in.shape[2]
    batches = heads_in.shape[1] // unit_rows
    shaped = heads_in.reshape(3, batches, unit_rows, local_width // HEAD, HEAD)
    return (shaped[0], shaped[1], shaped[2])


def masked_scores(query, keys, split_row):
    raw = jnp.einsum("sqhd,skhd->shqk", query, keys, preferred_element_type=jnp.float32) * HEAD ** (
        -0.5
    )
    row_pos = lax.broadcasted_iota(jnp.int32, raw.shape, 2)
    col_pos = lax.broadcasted_iota(jnp.int32, raw.shape, 3)
    same = (row_pos >= split_row) == (col_pos >= split_row)
    return jnp.where(same & (row_pos >= col_pos), raw, NEGATIVE)


def holder_pass(held_rows, gain_attn, gain_mlp, router, w_qkv, w_out, w_mlp, unit_rows, split_row):
    held_float = held_rows.astype(jnp.float32)
    scale_one = rms_scale(held_float)
    unit_one = held_float * scale_one
    normed_one = (unit_one * gain_attn).astype(jnp.bfloat16)
    gate = jax.nn.sigmoid(jnp.dot(held_float, router, precision=BEST))
    normed_all = lax.all_gather(normed_one, "mp", axis=0, tiled=True)
    heads_in = jnp.einsum(
        "rd,cde->cre", normed_all, w_qkv, preferred_element_type=jnp.float32
    ).astype(jnp.bfloat16)
    query, keys, values = split_heads(heads_in, unit_rows)
    scores = masked_scores(query, keys, split_row)
    peak = jnp.max(scores, axis=-1, keepdims=True)
    raised = jnp.exp(scores - peak)
    totals = jnp.sum(raised, axis=-1, keepdims=True)
    weights = (raised / totals).astype(jnp.bfloat16)
    log_total = peak + jnp.log(totals)
    mixed = jnp.einsum(
        "shqk,skhd->sqhd", weights, values, preferred_element_type=jnp.float32
    ).astype(jnp.bfloat16)
    mixed = mixed.reshape(normed_all.shape[0], heads_in.shape[2])
    attended = lax.psum_scatter(
        jnp.dot(mixed, w_out, preferred_element_type=jnp.float32),
        "mp",
        scatter_dimension=0,
        tiled=True,
    )
    middle = held_float + attended
    scale_two = rms_scale(middle)
    unit_two = middle * scale_two
    normed_two = (unit_two * gain_mlp).astype(jnp.bfloat16)
    normed_mid = lax.all_gather(normed_two, "mp", axis=0, tiled=True)
    upward = lax.dot_general(
        normed_mid, w_mlp[:, 0, :], CONTRACT_COLS, preferred_element_type=jnp.float32
    )
    active = gelu_tanh(upward).astype(jnp.bfloat16)
    feed = lax.psum_scatter(
        jnp.dot(active, w_mlp[:, 1, :], preferred_element_type=jnp.float32).astype(jnp.bfloat16),
        "mp",
        scatter_dimension=0,
        tiled=True,
    ).astype(jnp.float32)
    return (
        held_float,
        scale_one,
        unit_one,
        gate,
        normed_all,
        heads_in,
        log_total,
        mixed,
        attended,
        scale_two,
        unit_two,
        normed_mid,
        upward,
        active,
        attended + feed,
        w_mlp,
    )


def on_device(tokens, cotangent, lengths, routed, gain_attn, gain_mlp, router, w_qkv, w_out, w_mlp):
    group, span, width = tokens.shape
    slots = routed.shape[1]
    ranks = lax.axis_size("seq")
    held = group // ranks
    seq_rows = slots * ranks
    rows = held * seq_rows
    inner = routed % 8
    place = lax.axis_index("seq") * slots + lax.broadcasted_iota(jnp.int32, routed.shape, 1)
    live = place < (lengths // 8)[:, None]
    token_grid = tokens.reshape(group, slots, 8, width)
    grad_grid = cotangent.reshape(group, slots, 8, width)
    pick = lax.broadcasted_iota(jnp.int32, (group, slots, 8), 2) == inner[:, :, None]
    chosen = jnp.take_along_axis(token_grid, inner[:, :, None, None], axis=2)
    chosen_grad = jnp.take_along_axis(grad_grid, inner[:, :, None, None], axis=2)
    chosen_grad = jnp.where(live[:, :, None, None], chosen_grad, jnp.zeros_like(chosen_grad))
    got_tokens, got_grads = (
        lax.all_to_all(
            chosen.reshape(ranks, held, 1, slots, width),
            "seq",
            split_axis=0,
            concat_axis=2,
            tiled=True,
        ),
        lax.all_to_all(
            chosen_grad.reshape(ranks, held, 1, slots, width),
            "seq",
            split_axis=0,
            concat_axis=2,
            tiled=True,
        ),
    )
    held_rows = got_tokens.reshape(rows, width)
    held_grads = got_grads.reshape(rows, width)
    first_pass = holder_pass(
        held_rows, gain_attn, gain_mlp, router, w_qkv, w_out, w_mlp, seq_rows, seq_rows
    )
    returned = (first_pass[3][:, None] * first_pass[14]).astype(jnp.bfloat16)
    saved = holder_pass(
        held_rows, gain_attn, gain_mlp, router, w_qkv, w_out, w_mlp, seq_rows, seq_rows
    )
    (
        held_float,
        scale_one,
        unit_one,
        gate,
        normed_all,
        heads_in,
        log_total,
        mixed,
        attended,
        scale_two,
        unit_two,
        normed_mid,
        upward,
        active,
        delta,
        full_mlp,
    ) = saved
    grad_rows = held_grads.astype(jnp.float32)
    grad_logit = jnp.sum(grad_rows * delta, axis=-1) * gate * (1.0 - gate)
    router_part = jnp.dot(grad_logit, held_float, precision=BEST)
    grad_feed = (gate[:, None] * grad_rows).astype(jnp.bfloat16)
    feed_all = lax.all_gather(grad_feed, "mp", axis=0, tiled=True)
    grad_active = lax.dot_general(
        feed_all, w_mlp[:, 1, :], CONTRACT_COLS, preferred_element_type=jnp.float32
    )
    unused, gelu_pull = jax.vjp(gelu_tanh, upward)
    grad_upward = gelu_pull(grad_active)[0].astype(jnp.bfloat16)
    up_part = lax.dot_general(
        grad_upward, normed_mid, CONTRACT_ROWS, preferred_element_type=jnp.float32
    )
    down_part = lax.dot_general(active, feed_all, CONTRACT_ROWS, preferred_element_type=jnp.float32)
    mlp_local = jnp.stack([up_part, down_part], axis=1)
    grad_normed_two = lax.psum_scatter(
        jnp.dot(grad_upward, w_mlp[:, 0, :], preferred_element_type=jnp.float32),
        "mp",
        scatter_dimension=0,
        tiled=True,
    )
    grad_middle = norm_back(grad_normed_two, unit_two, scale_two, gain_mlp)
    mlp_gain_part = jnp.sum(grad_normed_two * unit_two, axis=0)
    grad_attended = (gate[:, None] * grad_rows + grad_middle).astype(jnp.bfloat16)
    attended_all = lax.all_gather(grad_attended, "mp", axis=0, tiled=True)
    out_local = lax.dot_general(
        mixed, attended_all, CONTRACT_ROWS, preferred_element_type=jnp.float32
    )
    grad_mixed = lax.dot_general(
        attended_all, w_out, CONTRACT_COLS, preferred_element_type=jnp.float32
    ).astype(jnp.bfloat16)
    query, keys, values = split_heads(heads_in, seq_rows)
    grad_heads_mixed = grad_mixed.reshape(query.shape)
    scores = masked_scores(query, keys, seq_rows)
    shares = jnp.exp(scores - log_total)
    weights = shares.astype(jnp.bfloat16)
    grad_weights = jnp.einsum(
        "sqhd,skhd->shqk", grad_heads_mixed, values, preferred_element_type=jnp.float32
    )
    grad_scores = (
        shares * (grad_weights - jnp.sum(shares * grad_weights, axis=-1, keepdims=True))
    ).astype(jnp.bfloat16)
    grad_query = jnp.einsum(
        "shqk,skhd->sqhd", grad_scores, keys, preferred_element_type=jnp.float32
    ) * HEAD ** (-0.5)
    grad_keys = jnp.einsum(
        "shqk,sqhd->skhd", grad_scores, query, preferred_element_type=jnp.float32
    ) * HEAD ** (-0.5)
    grad_values = jnp.einsum(
        "shqk,sqhd->skhd", weights, grad_heads_mixed, preferred_element_type=jnp.float32
    )
    grad_heads = (
        jnp.stack([grad_query, grad_keys, grad_values]).astype(jnp.bfloat16).reshape(heads_in.shape)
    )
    qkv_local = jnp.einsum(
        "rd,cre->cde", normed_all, grad_heads, preferred_element_type=jnp.float32
    )
    grad_normed_one = lax.psum_scatter(
        jnp.einsum("cre,cde->rd", grad_heads, w_qkv, preferred_element_type=jnp.float32).astype(
            jnp.bfloat16
        ),
        "mp",
        scatter_dimension=0,
        tiled=True,
    ).astype(jnp.float32)
    attn_gain_part = jnp.sum(grad_normed_one * unit_one, axis=0)
    grad_picked = (
        grad_middle
        + norm_back(grad_normed_one, unit_one, scale_one, gain_attn)
        + grad_logit[:, None] * router
    ).astype(jnp.bfloat16)
    back_out, back_grad = (
        lax.all_to_all(
            returned.reshape(1, held, ranks, slots, width),
            "seq",
            split_axis=2,
            concat_axis=0,
            tiled=True,
        ),
        lax.all_to_all(
            grad_picked.reshape(1, held, ranks, slots, width),
            "seq",
            split_axis=2,
            concat_axis=0,
            tiled=True,
        ),
    )
    keep = pick[:, :, :, None] & live[:, :, None, None]
    back_out = back_out.reshape(group, slots, 1, width).astype(jnp.float32)
    back_grad = back_grad.reshape(group, slots, 1, width).astype(jnp.float32)
    layer_out = (token_grid.astype(jnp.float32) + jnp.where(keep, back_out, 0.0)).astype(
        jnp.bfloat16
    )
    grad_tokens = (grad_grid.astype(jnp.float32) + jnp.where(keep, back_grad, 0.0)).astype(
        jnp.bfloat16
    )
    grad_qkv, grad_out, grad_mlp = (
        lax.psum(qkv_local.astype(jnp.bfloat16), "seq").astype(jnp.float32),
        lax.psum(out_local.astype(jnp.bfloat16), "seq").astype(jnp.float32),
        lax.psum(mlp_local.astype(jnp.bfloat16), "seq").astype(jnp.float32),
    )
    grad_gain_attn, grad_gain_mlp, grad_router = lax.psum(
        (attn_gain_part, mlp_gain_part, router_part), ("seq", "mp")
    )
    return (
        layer_out.reshape(group, span, width),
        grad_tokens.reshape(group, span, width),
        grad_gain_attn,
        grad_gain_mlp,
        grad_router,
        grad_qkv,
        grad_out,
        grad_mlp,
    )


def solution(mesh):
    placed = (
        P("mp", "seq", None),
        P("mp", "seq", None),
        P("mp"),
        P("mp", "seq"),
        P(),
        P(),
        P(),
        P(None, None, "mp"),
        P("mp", None),
        P("mp", None, None),
    )
    return jax.shard_map(
        on_device,
        mesh=mesh,
        in_specs=placed,
        out_specs=(
            P("mp", "seq", None),
            P("mp", "seq", None),
            P(),
            P(),
            P(),
            P(None, None, "mp"),
            P("mp", None),
            P("mp", None, None),
        ),
        check_vma=False,
    )
```

profile of v0, /device:TPU:0, one launch (start us, length us, event | category | flops | bytes accessed | tf_op | source)
XLA Modules:
  0.0 1143.7 jit_solution(17167783072121866484)
XLA Ops:
  9.4 8.4 gather_fusion.1
  17.9 8.4 gather_fusion
  29.2 20.3 %all_to_all.42 = bf16[8,2,1,32,1024]{4,3,1,2,0:T(8,128)(2,1)S(1)} all-to-all(bf16[8,2,1,32,1024]{4,3,1,2,0:T(8,128)(2,1)S(1)} %bitcast.192), channel_id=1, replica_groups=mesh['seq'=8,'mp'=4] {'seq'}, dimensions={0} | all-to-all | bytes 2097152 | tf_op jit(solution)/shard_map/all_to_all | solution.py:123
  53.2 80.2 %all-gather.5.cloned.1.call-done = bf16[2048,1024]{1,0:T(8,128)(2,1)} async-done(((bf16[512,1024]{1,0:T(8,128)(2,1)}), bf16[2048,1024]{1,0:T(8,128)(2,1)}) %all-gather.5.cloned.1.call-update) | async-done | bytes 4194320 | tf_op jit(solution)/shard_map/all_gather | solution.py:50
  181.6 143.1 %reduce-scatter.5.cloned.1.call-done = f32[512,1024]{1,0:T(8,128)} async-done(((f32[2048,1024]{1,0:T(8,128)}), f32[512,1024]{1,0:T(8,128)}) %reduce-scatter.5.cloned.1.call-update) | async-done | bytes 2097168 | tf_op jit(solution)/shard_map/reduce_scatter | solution.py:65
  328.4 19.2 %all_to_all.43 = bf16[8,2,1,32,1024]{4,3,1,2,0:T(8,128)(2,1)S(1)} all-to-all(bf16[8,2,1,32,1024]{4,3,1,2,0:T(8,128)(2,1)} %bitcast.191), channel_id=1, replica_groups=mesh['seq'=8,'mp'=4] {'seq'}, dimensions={0} | all-to-all | bytes 2097152 | tf_op jit(solution)/shard_map/all_to_all | solution.py:130
  350.7 10.2 fusion.69
  360.9 49.1 %all-gather.7.cloned.1.call-done = bf16[2048,1024]{1,0:T(8,128)(2,1)} async-done(((bf16[512,1024]{1,0:T(8,128)(2,1)}), bf16[2048,1024]{1,0:T(8,128)(2,1)}) %all-gather.7.cloned.1.call-update) | async-done | bytes 4194320 | tf_op jit(solution)/shard_map/all_gather | solution.py:75
  410.0 10.3 fusion.58
  423.7 7.2 convolution_convert_fusion
  431.0 60.3 %all-gather.9.cloned.1.call-done = bf16[2048,1024]{1,0:T(8,128)(2,1)} async-done(((bf16[512,1024]{1,0:T(8,128)(2,1)}), bf16[2048,1024]{1,0:T(8,128)(2,1)}) %all-gather.9.cloned.1.call-update) | async-done | bytes 4194320 | tf_op jit(solution)/shard_map/all_gather | solution.py:169
  491.3 14.6 %fusion.10 = bf16[2048,1024]{1,0:T(8,128)(2,1)S(1)} fusion(f32[2048,1024]{1,0:T(8,128)} %copy-done.36, bf16[2048,1024]{1,0:T(8,128)(2,1)} %all-gather.9.cloned.1.call-done, bf16[1024,1,1024]{2,1,0:T(2,128)(2,1)} %get-tuple-element.63), kind=kOutput, calls=%fused_computation.16 | convolution fusion | flops 4336910336 | bytes 18874368 | tf_op jit(solution)/shard_map/dot_general | solution.py:170
  507.9 6.9 fusion.57
  514.8 54.0 %reduce-scatter.7.cloned.1.call-done = bf16[512,1024]{1,0:T(8,128)(2,1)} async-done(((bf16[2048,1024]{1,0:T(8,128)(2,1)}), bf16[512,1024]{1,0:T(8,128)(2,1)}) %reduce-scatter.7.cloned.1.call-update) | async-done | bytes 1048592 | tf_op jit(solution)/shard_map/reduce_scatter | solution.py:80
  568.8 147.9 %reduce-scatter.9.cloned.1.call-done = f32[512,1024]{1,0:T(8,128)} async-done(((f32[2048,1024]{1,0:T(8,128)}), f32[512,1024]{1,0:T(8,128)}) %reduce-scatter.9.cloned.1.call-update) | async-done | bytes 2097168 | tf_op jit(solution)/shard_map/reduce_scatter | solution.py:180
  723.9 81.6 %all-gather.11.cloned.1.call-done = bf16[2048,1024]{1,0:T(8,128)(2,1)} async-done(((bf16[512,1024]{1,0:T(8,128)(2,1)}), bf16[2048,1024]{1,0:T(8,128)(2,1)}) %all-gather.11.cloned.1.call-update) | async-done | bytes 4194320 | tf_op jit(solution)/shard_map/all_gather | solution.py:189
  818.5 6.3 fusion.52
  871.4 8.2 convert_bitcast_fusion.2
  879.6 9.0 convert_bitcast_fusion.1
  907.3 39.2 %reduce-scatter.11.cloned.1.call-done = bf16[512,1024]{1,0:T(8,128)(2,1)} async-done(((bf16[2048,1024]{1,0:T(8,128)(2,1)}), bf16[512,1024]{1,0:T(8,128)(2,1)}) %reduce-scatter.11.cloned.1.call-update) | async-done | bytes 1048592 | tf_op jit(solution)/shard_map/reduce_scatter | solution.py:222
  961.1 106.0 %all-reduce.4.cloned.1.call-done = (bf16[3,1024,256]{1,2,0:T(8,128)(2,1)}, bf16[1024,2,1024]{2,0,1:T(8,128)(2,1)}, bf16[256,1024]{1,0:T(8,128)(2,1)}) async-done(((bf16[3,1024,256]{1,2,0:T(8,128)(2,1)}, bf16[1024,2,1024]{2,0,1:T(8,128)(2,1)}, bf16[256,1024]{1,0:T(8,128)(2,1)}), (bf16[3,1024,256]{1,2,0:T(8,128)(2,1)}, bf16[1024,2,1024]{2,0,1:T(8,128)(2,1)}, ...) | async-done | bytes 6291472 | tf_op jit(solution)/shard_map/psum | solution.py:262
  1072.2 9.9 copy.186
  1082.1 39.6 %all-reduce = (f32[1024]{0:T(1024)}, f32[1024]{0:T(1024)}, f32[1024]{0:T(1024)}) all-reduce(f32[1024]{0:T(1024)S(1)} %get-tuple-element.51, f32[1024]{0:T(1024)S(1)} %get-tuple-element.49, f32[1024]{0:T(1024)S(1)} %bitcast.204), channel_id=1, replica_groups=mesh['seq'=8,'mp'=4] {'seq','mp'}, use_global_device_ids=true, to_apply=%region_13.15 | all-reduce | flops 3072 | bytes 24576 | tf_op jit(solution)/shard_map/psum | solution.py:266
  1123.6 13.1 %fusion.1 = (bf16[16,256,1024]{2,1,0:T(8,128)(2,1)}, bf16[16,256,1024]{2,1,0:T(8,128)(2,1)}) fusion(bf16[16,256,1024]{2,1,0:T(8,128)(2,1)} %param.13, f32[16,32,1024]{2,1,0:T(8,128)S(1)} %bitcast.185, pred[16,256]{1,0:T(8,128)(4,1)S(1)} %copy.149, f32[16,32,1024]{2,1,0:T(8,128)S(1)} %bitcast.184, bf16[16,256,1024]{2,1,0:T(8,128)(2,1)} %param.12), kind=kLoop, calls=%fused_computation.4 | loop fusion | flops 33554432 | bytes 37752832 | tf_op jit(solution)/shard_map/convert_element_type | solution.py:258
  (181 shorter events, 175.8 us)
Async XLA Ops:
  7.2 126.3 %copy-start = (bf16[3,1024,256]{2,1,0:T(8,128)(2,1)S(1)}, bf16[3,1024,256]{2,1,0:T(8,128)(2,1)}, u32[]{:S(2)}) copy-start(bf16[3,1024,256]{2,1,0:T(8,128)(2,1)} %param.19) | copy-start | bytes 4718596
  7.2 126.2 %all-gather.5.cloned.1.call-start = ((), (), s32[]{:S(2)}) async-start(), calls=%async_computation.8 | async-start | bytes 5242880 | tf_op jit(solution)/shard_map/all_gather | solution.py:50
  26.4 25.4 %copy-start.25 = (f32[1024]{0:T(1024)S(1)}, f32[1024]{0:T(1024)}, u32[]{:S(2)}) copy-start(f32[1024]{0:T(1024)} %param.16) | copy-start | bytes 12292
  50.5 88.6 %copy-start.27 = (f32[512]{0:T(512)}, f32[512]{0:T(512)S(1)}, u32[]{:S(2)}) copy-start(f32[512]{0:T(512)S(1)} %rsqrt.22) | copy-start | bytes 6148
  53.1 271.6 %reduce-scatter.5.cloned.1.call-start = ((), (), s32[]{:S(2)}) async-start(), calls=%async_computation.9 | async-start | bytes 10485760 | tf_op jit(solution)/shard_map/reduce_scatter | solution.py:65
  181.5 145.3 %copy-start.24 = (f32[1024]{0:T(1024)S(1)}, f32[1024]{0:T(1024)}, u32[]{:S(2)}) copy-start(f32[1024]{0:T(1024)} %param.17) | copy-start | bytes 12292
  181.6 228.4 %all-gather.7.cloned.1.call-start = ((), (), s32[]{:S(2)}) async-start(), calls=%async_computation.10 | async-start | bytes 5242880 | tf_op jit(solution)/shard_map/all_gather | solution.py:75
  328.3 163.0 %all-gather.9.cloned.1.call-start = ((), (), s32[]{:S(2)}) async-start(), calls=%async_computation.12 | async-start | bytes 5242880 | tf_op jit(solution)/shard_map/all_gather | solution.py:169
  350.6 218.2 %reduce-scatter.7.cloned.1.call-start = ((), (), s32[]{:S(2)}) async-start(), calls=%async_computation.11 | async-start | bytes 5242880 | tf_op jit(solution)/shard_map/reduce_scatter | solution.py:80
  410.0 13.7 %copy-start.18 = (bf16[1024,1,1024]{2,1,0:T(2,128)(2,1)S(1)}, bf16[1024,1,1024]{2,1,0:T(2,128)(2,1)}, u32[]{:S(2)}) copy-start(bf16[1024,1,1024]{2,1,0:T(2,128)(2,1)} %get-tuple-element.63) | copy-start | bytes 6291460
  430.9 285.8 %reduce-scatter.9.cloned.1.call-start = ((), (), s32[]{:S(2)}) async-start(), calls=%async_computation.13 | async-start | bytes 10485760 | tf_op jit(solution)/shard_map/reduce_scatter | solution.py:180
  491.3 16.5 %copy-start.17 = (bf16[1024,1,1024]{2,1,0:T(2,128)(2,1)S(1)}, bf16[1024,1,1024]{2,1,0:T(2,128)(2,1)}, u32[]{:S(2)}) copy-start(bf16[1024,1,1024]{2,1,0:T(2,128)(2,1)} %get-tuple-element.62) | copy-start | bytes 6291460
  514.8 290.7 %all-gather.11.cloned.1.call-start = ((), (), s32[]{:S(2)}) async-start(), calls=%async_computation.14 | async-start | bytes 5242880 | tf_op jit(solution)/shard_map/all_gather | solution.py:189
  723.9 222.7 %reduce-scatter.11.cloned.1.call-start = ((), (), s32[]{:S(2)}) async-start(), calls=%async_computation.15 | async-start | bytes 5242880 | tf_op jit(solution)/shard_map/reduce_scatter | solution.py:222
  818.5 6.3 copy-start.14
  818.5 11.9 %slice-start = ((s8[8388608]{0:T(1024)(128)(4,1)}), s8[4194304]{0:T(1024)(128)(4,1)S(1)}, s32[]{:S(2)}) async-start(s8[8388608]{0:T(1024)(128)(4,1)} %bitcast.177), calls=%async_computation.17 | async-start | bytes 8388608
  871.1 195.9 %all-reduce.4.cloned.1.call-start = ((), (), s32[]{:S(2)}) async-start(), calls=%async_computation.16 | async-start | bytes 12582912 | tf_op jit(solution)/shard_map/psum | solution.py:262
  871.4 8.2 copy-start.33
  900.5 46.1 %copy-start.26 = (f32[1024]{0:T(1024)S(1)}, f32[1024]{0:T(1024)}, u32[]{:S(2)}) copy-start(f32[1024]{0:T(1024)} %param.16) | copy-start | bytes 12292
  900.5 46.1 %copy-start.28 = (f32[512]{0:T(512)S(1)}, f32[512]{0:T(512)}, u32[]{:S(2)}) copy-start(f32[512]{0:T(512)} %copy-done.27) | copy-start | bytes 6148
  902.8 50.2 %all-to-all-start.1 = ((bf16[1,2,8,32,1024]{4,3,1,0,2:T(8,128)(2,1)}), bf16[1,2,8,32,1024]{4,3,1,0,2:T(8,128)(2,1)}, u32[]{:S(2)}, u32[]{:S(2)}) async-start(bf16[1,2,8,32,1024]{4,3,1,0,2:T(8,128)(2,1)} %copy.163), calls=%async_computation.3 | async-start | bytes 2097152 | tf_op jit(solution)/shard_map/all_to_all | solution.py:237
  948.6 8.6 copy-start.30
  948.6 8.7 copy-start.23
  953.0 168.7 %all-to-all-start.3 = ((bf16[1,2,8,32,1024]{4,3,1,0,2:T(8,128)(2,1)}), bf16[1,2,8,32,1024]{4,3,1,0,2:T(8,128)(2,1)}, u32[]{:S(2)}, u32[]{:S(2)}) async-start(bf16[1,2,8,32,1024]{4,3,1,0,2:T(8,128)(2,1)} %copy.182), calls=%async_computation.7 | async-start | bytes 2097152 | tf_op jit(solution)/shard_map/all_to_all | solution.py:244
  (26 other events, 74.2 us)
Sparse Core Ops, SparseCore 0:
  53.3 80.1 all-gather.4
  181.7 143.0 reduce-scatter.4
  328.5 81.4 all-gather.6
  412.0 79.2 all-gather.8
  493.4 75.3 reduce-scatter.6
  571.7 144.9 reduce-scatter.8
  724.0 81.4 all-gather.10
  871.3 75.2 reduce-scatter.10
  950.7 116.3 all-reduce.3
where the time goes:
time: 1150 us; the launch traced here: 1140 us
  waiting for transfers between devices  762 us (66%)
  local copies, waits for them, and re-layouts  124 us (11%)
  matrix products  106 us (9%)
  blocking collectives  79.1 us (7%)
  other arithmetic  49.2 us (4%)
  between operations  14.8 us (1%)
    reduce_scatter x1, waiting for transfers between devices, on_device(): lax.psum_scatter(jnp.dot(grad_upward, w_mlp[:, 0, :], preferred_element_t...  148 us
    reduce_scatter x1, waiting for transfers between devices, holder_pass(): lax.psum_scatter(jnp.dot(mixed, w_out, preferred_element_type=jnp.float32...  143 us
    psum x1, waiting for transfers between devices, on_device(): lax.psum(qkv_local.astype(jnp.bfloat16), 'seq').astype(jnp.float32)  106 us
    all_gather x1, waiting for transfers between devices, on_device(): attended_all = lax.all_gather(grad_attended, 'mp', axis=0, tiled=True)  81.6 us
    all_gather x1, waiting for transfers between devices, holder_pass(): normed_all = lax.all_gather(normed_one, 'mp', axis=0, tiled=True)  80.2 us
    all_gather x1, waiting for transfers between devices, on_device(): feed_all = lax.all_gather(grad_feed, 'mp', axis=0, tiled=True)  60.3 us
    reduce_scatter x1, waiting for transfers between devices, holder_pass(): lax.psum_scatter(jnp.dot(active, w_mlp[:, 1, :], preferred_element_type=j...  54 us
    all_gather x1, waiting for transfers between devices, holder_pass(): normed_mid = lax.all_gather(normed_two, 'mp', axis=0, tiled=True)  49.1 us
  transfers between devices with their start and end apart: 11, of which 9 were waited for; matrix products, arithmetic and copies ran while one was open for 9% of the time, Pallas kernels for 0%

commit v1 on v0

--- a/solution.py
+++ b/solution.py
@@ -166,7 +166,18 @@
     grad_logit = jnp.sum(grad_rows * delta, axis=-1) * gate * (1.0 - gate)
     router_part = jnp.dot(grad_logit, held_float, precision=BEST)
     grad_feed = (gate[:, None] * grad_rows).astype(jnp.bfloat16)
-    feed_all = lax.all_gather(grad_feed, "mp", axis=0, tiled=True)
+    devices, index, rows_2 = (lax.axis_size("mp"), lax.axis_index("mp"), grad_feed.shape[0])
+    right = [(i, (i + 1) % devices) for i in range(devices)]
+    out = jnp.zeros(
+        (*grad_feed.shape[:0], devices * rows_2, *grad_feed.shape[0 + 1 :]), grad_feed.dtype
+    )
+    carried = grad_feed
+    for turn in range(devices):
+        source = (index - turn) % devices
+        out = lax.dynamic_update_slice_in_dim(out, carried, source * rows_2, axis=0)
+        if turn < devices - 1:
+            carried = lax.ppermute(carried, "mp", right)
+    feed_all = out
     grad_active = lax.dot_general(
         feed_all, w_mlp[:, 1, :], CONTRACT_COLS, preferred_element_type=jnp.float32
     )

time: 1150 us -> 1180 us (1.026)
  starting transfers between devices: 9.33 us -> 33.4 us
  blocking collectives: 79.1 us -> 59.9 us
  waiting for transfers between devices: 762 us -> 776 us
    ppermute x0 -> x3, waiting for transfers between devices: none -> 95.4 us  [on_device(): carried = lax.ppermute(carried, 'mp', right)]
    all_gather x1 -> x0, waiting for transfers between devices: 60.3 us -> none  [on_device(): feed_all = lax.all_gather(grad_feed, 'mp', axis=0, tiled=True)]
    reduce_scatter x1, waiting for transfers between devices: 54 us -> 0.02 us  [holder_pass(): lax.psum_scatter(jnp.dot(active, w_mlp[:, 1, :], preferred_element_type=j...]
    all_gather x1, waiting for transfers between devices: 49.1 us -> 71.2 us  [holder_pass(): normed_mid = lax.all_gather(normed_two, 'mp', axis=0, tiled=True)]
    ppermute x0 -> x3, starting transfers between devices: none -> 19.9 us  [on_device(): carried = lax.ppermute(carried, 'mp', right)]
    all_to_all x1 -> x0, blocking collectives: 19.2 us -> none  [on_device(): lax.all_to_all(chosen_grad.reshape(ranks, held, 1, slots, width), 'seq',...]
    all_to_all x0 -> x1, waiting for transfers between devices: none -> 15.3 us  [on_device(): lax.all_to_all(chosen_grad.reshape(ranks, held, 1, slots, width), 'seq',...]
    unnamed x83 -> x89, local copies, waits for them, and re-layouts: 30.4 us -> 32.9 us
  transfers between devices with their start and end apart: 11 -> 14, of which waited for: 9 -> 11; matrix products, arithmetic and copies ran while one was open for 9% -> 8% of each run, Pallas kernels for 0% -> 0%
where the time goes in v1:
time: 1180 us; the launch traced here: 1170 us
  waiting for transfers between devices  776 us (66%)
  local copies, waits for them, and re-layouts  135 us (11%)
  matrix products  104 us (9%)
  blocking collectives  59.9 us (5%)
  other arithmetic  49.5 us (4%)
  starting transfers between devices  33.4 us (3%)
  between operations  14.9 us (1%)
    reduce_scatter x1, waiting for transfers between devices, on_device(): lax.psum_scatter(jnp.dot(grad_upward, w_mlp[:, 0, :], preferred_element_t...  144 us
    reduce_scatter x1, waiting for transfers between devices, holder_pass(): lax.psum_scatter(jnp.dot(mixed, w_out, preferred_element_type=jnp.float32...  143 us
    psum x1, waiting for transfers between devices, on_device(): lax.psum(qkv_local.astype(jnp.bfloat16), 'seq').astype(jnp.float32)  106 us
    ppermute x3, waiting for transfers between devices, on_device(): carried = lax.ppermute(carried, 'mp', right)  95.4 us
    all_gather x1, waiting for transfers between devices, on_device(): attended_all = lax.all_gather(grad_attended, 'mp', axis=0, tiled=True)  81.6 us
    all_gather x1, waiting for transfers between devices, holder_pass(): normed_all = lax.all_gather(normed_one, 'mp', axis=0, tiled=True)  80.2 us
    all_gather x1, waiting for transfers between devices, holder_pass(): normed_mid = lax.all_gather(normed_two, 'mp', axis=0, tiled=True)  71.2 us
    psum x1, blocking collectives, on_device(): lax.psum((attn_gain_part, mlp_gain_part, router_part), ('seq', 'mp'))  39.6 us
  transfers between devices with their start and end apart: 14, of which 11 were waited for; matrix products, arithmetic and copies ran while one was open for 8% of the time, Pallas kernels for 0%

profile of v1, /device:TPU:0, one launch (start us, length us, event | category | flops | bytes accessed | tf_op | source)
XLA Modules:
  0.0 1172.3 jit_solution(4361416221310719776)
XLA Ops:
  9.4 8.4 gather_fusion.1
  17.9 8.4 gather_fusion
  29.2 20.3 %all_to_all.42 = bf16[8,2,1,32,1024]{4,3,1,2,0:T(8,128)(2,1)S(1)} all-to-all(bf16[8,2,1,32,1024]{4,3,1,2,0:T(8,128)(2,1)S(1)} %bitcast.192), channel_id=1, replica_groups=mesh['seq'=8,'mp'=4] {'seq'}, dimensions={0} | all-to-all | bytes 2097152 | tf_op jit(solution)/shard_map/all_to_all | solution.py:123
  53.2 80.2 %all-gather.4.cloned.1.call-done = bf16[2048,1024]{1,0:T(8,128)(2,1)} async-done(((bf16[512,1024]{1,0:T(8,128)(2,1)}), bf16[2048,1024]{1,0:T(8,128)(2,1)}) %all-gather.4.cloned.1.call-update) | async-done | bytes 4194320 | tf_op jit(solution)/shard_map/all_gather | solution.py:50
  181.9 143.1 %reduce-scatter.5.cloned.1.call-done = f32[512,1024]{1,0:T(8,128)} async-done(((f32[2048,1024]{1,0:T(8,128)}), f32[512,1024]{1,0:T(8,128)}) %reduce-scatter.5.cloned.1.call-update) | async-done | bytes 2097168 | tf_op jit(solution)/shard_map/reduce_scatter | solution.py:65
  328.7 10.4 fusion.69
  339.0 71.2 %all-gather.6.cloned.1.call-done = bf16[2048,1024]{1,0:T(8,128)(2,1)} async-done(((bf16[512,1024]{1,0:T(8,128)(2,1)}), bf16[2048,1024]{1,0:T(8,128)(2,1)}) %all-gather.6.cloned.1.call-update) | async-done | bytes 4194320 | tf_op jit(solution)/shard_map/all_gather | solution.py:75
  410.2 10.3 fusion.58
  424.0 7.3 convolution_convert_fusion
  435.6 15.3 %all-to-all-done.2 = bf16[8,2,1,32,1024]{4,3,1,2,0:T(8,128)(2,1)} async-done(((bf16[8,2,1,32,1024]{4,3,1,2,0:T(8,128)(2,1)}), bf16[8,2,1,32,1024]{4,3,1,2,0:T(8,128)(2,1)}, u32[]{:S(2)}, u32[]{:S(2)}) %all-to-all-start.2) | async-done | bytes 1048608 | tf_op jit(solution)/shard_map/all_to_all | solution.py:130
  456.4 48.9 %collective-permute-done = bf16[512,1024]{1,0:T(8,128)(2,1)S(1)} collective-permute-done((bf16[512,1024]{1,0:T(8,128)(2,1)S(1)}, bf16[512,1024]{1,0:T(8,128)(2,1)S(1)}, u32[]{:S(2)}, u32[]{:S(2)}) %collective-permute-start) | collective-permute-done | bytes 1048608 | tf_op jit(solution)/shard_map/ppermute | solution.py:179
  506.3 19.9 %collective-permute-start.1 = (bf16[512,1024]{1,0:T(8,128)(2,1)S(1)}, bf16[512,1024]{1,0:T(8,128)(2,1)}, u32[]{:S(2)}, u32[]{:S(2)}) collective-permute-start(bf16[512,1024]{1,0:T(8,128)(2,1)S(1)} %collective-permute-done), channel_id=1, source_target_pairs={{0,1},{1,2},{2,3},{3,0},{4,5},{5,6},{6,7},{7,4},{8,9},{9,10},{10,1... | collective-permute-start | bytes 3145736 | tf_op jit(solution)/shard_map/ppermute | solution.py:179
  526.1 26.4 %collective-permute-done.1 = bf16[512,1024]{1,0:T(8,128)(2,1)} collective-permute-done((bf16[512,1024]{1,0:T(8,128)(2,1)S(1)}, bf16[512,1024]{1,0:T(8,128)(2,1)}, u32[]{:S(2)}, u32[]{:S(2)}) %collective-permute-start.1) | collective-permute-done | bytes 1048608 | tf_op jit(solution)/shard_map/ppermute | solution.py:179
  557.3 20.1 %collective-permute-done.2 = bf16[512,1024]{1,0:T(8,128)(2,1)} collective-permute-done((bf16[512,1024]{1,0:T(8,128)(2,1)}, bf16[512,1024]{1,0:T(8,128)(2,1)}, u32[]{:S(2)}, u32[]{:S(2)}) %collective-permute-start.2) | collective-permute-done | bytes 1048608 | tf_op jit(solution)/shard_map/ppermute | solution.py:179
  579.6 12.6 %fusion.10 = bf16[2048,1024]{1,0:T(8,128)(2,1)S(1)} fusion(f32[2048,1024]{1,0:T(8,128)} %copy-done.39, bf16[2048,1024]{1,0:T(8,128)(2,1)} %constant_dynamic-update-slice_fusion.3, bf16[1024,1,1024]{2,1,0:T(2,128)(2,1)S(1)} %copy-done.21), kind=kOutput, calls=%fused_computation.16 | convolution fusion | flops 4336910336 | bytes 18874368 | tf_op jit(solution)/shard_map/dot_general | solution.py:181
  601.2 143.9 %reduce-scatter.9.cloned.1.call-done = f32[512,1024]{1,0:T(8,128)} async-done(((f32[2048,1024]{1,0:T(8,128)}), f32[512,1024]{1,0:T(8,128)}) %reduce-scatter.9.cloned.1.call-update) | async-done | bytes 2097168 | tf_op jit(solution)/shard_map/reduce_scatter | solution.py:191
  752.3 81.6 %all-gather.8.cloned.1.call-done = bf16[2048,1024]{1,0:T(8,128)(2,1)} async-done(((bf16[512,1024]{1,0:T(8,128)(2,1)}), bf16[2048,1024]{1,0:T(8,128)(2,1)}) %all-gather.8.cloned.1.call-update) | async-done | bytes 4194320 | tf_op jit(solution)/shard_map/all_gather | solution.py:200
  899.9 8.2 convert_bitcast_fusion.2
  908.1 9.0 convert_bitcast_fusion.1
  935.8 39.3 %reduce-scatter.11.cloned.1.call-done = bf16[512,1024]{1,0:T(8,128)(2,1)} async-done(((bf16[2048,1024]{1,0:T(8,128)(2,1)}), bf16[512,1024]{1,0:T(8,128)(2,1)}) %reduce-scatter.11.cloned.1.call-update) | async-done | bytes 1048592 | tf_op jit(solution)/shard_map/reduce_scatter | solution.py:233
  989.6 105.9 %all-reduce.4.cloned.1.call-done = (bf16[3,1024,256]{1,2,0:T(8,128)(2,1)}, bf16[1024,2,1024]{2,0,1:T(8,128)(2,1)}, bf16[256,1024]{1,0:T(8,128)(2,1)}) async-done(((bf16[3,1024,256]{1,2,0:T(8,128)(2,1)}, bf16[1024,2,1024]{2,0,1:T(8,128)(2,1)}, bf16[256,1024]{1,0:T(8,128)(2,1)}), (bf16[3,1024,256]{1,2,0:T(8,128)(2,1)}, bf16[1024,2,1024]{2,0,1:T(8,128)(2,1)}, ...) | async-done | bytes 6291472 | tf_op jit(solution)/shard_map/psum | solution.py:273
  1100.8 9.9 copy.186
  1110.7 39.6 %all-reduce = (f32[1024]{0:T(1024)}, f32[1024]{0:T(1024)}, f32[1024]{0:T(1024)}) all-reduce(f32[1024]{0:T(1024)S(1)} %get-tuple-element.51, f32[1024]{0:T(1024)S(1)} %get-tuple-element.49, f32[1024]{0:T(1024)S(1)} %bitcast.204), channel_id=1, replica_groups=mesh['seq'=8,'mp'=4] {'seq','mp'}, use_global_device_ids=true, to_apply=%region_13.15 | all-reduce | flops 3072 | bytes 24576 | tf_op jit(solution)/shard_map/psum | solution.py:277
  1152.1 13.1 %fusion.1 = (bf16[16,256,1024]{2,1,0:T(8,128)(2,1)}, bf16[16,256,1024]{2,1,0:T(8,128)(2,1)}) fusion(bf16[16,256,1024]{2,1,0:T(8,128)(2,1)} %param.13, f32[16,32,1024]{2,1,0:T(8,128)S(1)} %bitcast.185, pred[16,256]{1,0:T(8,128)(4,1)S(1)} %copy.149, f32[16,32,1024]{2,1,0:T(8,128)S(1)} %bitcast.184, bf16[16,256,1024]{2,1,0:T(8,128)(2,1)} %param.12), kind=kLoop, calls=%fused_computation.4 | loop fusion | flops 33554432 | bytes 37752832 | tf_op jit(solution)/shard_map/convert_element_type | solution.py:269
  (195 shorter events, 204.0 us)
Async XLA Ops:
  7.2 126.3 %copy-start = (bf16[3,1024,256]{2,1,0:T(8,128)(2,1)S(1)}, bf16[3,1024,256]{2,1,0:T(8,128)(2,1)}, u32[]{:S(2)}) copy-start(bf16[3,1024,256]{2,1,0:T(8,128)(2,1)} %param.19) | copy-start | bytes 4718596
  7.2 126.2 %all-gather.4.cloned.1.call-start = ((), (), s32[]{:S(2)}) async-start(), calls=%async_computation.8 | async-start | bytes 5242880 | tf_op jit(solution)/shard_map/all_gather | solution.py:50
  26.4 25.4 %copy-start.29 = (f32[1024]{0:T(1024)S(1)}, f32[1024]{0:T(1024)}, u32[]{:S(2)}) copy-start(f32[1024]{0:T(1024)} %param.16) | copy-start | bytes 12292
  50.5 88.6 %copy-start.31 = (f32[512]{0:T(512)}, f32[512]{0:T(512)S(1)}, u32[]{:S(2)}) copy-start(f32[512]{0:T(512)S(1)} %rsqrt.22) | copy-start | bytes 6148
  53.1 271.9 %reduce-scatter.5.cloned.1.call-start = ((), (), s32[]{:S(2)}) async-start(), calls=%async_computation.9 | async-start | bytes 10485760 | tf_op jit(solution)/shard_map/reduce_scatter | solution.py:65
  181.8 145.3 %copy-start.28 = (f32[1024]{0:T(1024)S(1)}, f32[1024]{0:T(1024)}, u32[]{:S(2)}) copy-start(f32[1024]{0:T(1024)} %param.17) | copy-start | bytes 12292
  181.8 228.4 %all-gather.6.cloned.1.call-start = ((), (), s32[]{:S(2)}) async-start(), calls=%async_computation.10 | async-start | bytes 5242880 | tf_op jit(solution)/shard_map/all_gather | solution.py:75
  328.6 272.6 %reduce-scatter.7.cloned.1.call-start = ((), (), s32[]{:S(2)}) async-start(), calls=%async_computation.11 | async-start | bytes 5242880 | tf_op jit(solution)/shard_map/reduce_scatter | solution.py:80
  410.2 13.7 %copy-start.20 = (bf16[1024,1,1024]{2,1,0:T(2,128)(2,1)S(1)}, bf16[1024,1,1024]{2,1,0:T(2,128)(2,1)}, u32[]{:S(2)}) copy-start(bf16[1024,1,1024]{2,1,0:T(2,128)(2,1)} %get-tuple-element.63) | copy-start | bytes 6291460
  431.3 19.7 %all-to-all-start.2 = ((bf16[8,2,1,32,1024]{4,3,1,2,0:T(8,128)(2,1)}), bf16[8,2,1,32,1024]{4,3,1,2,0:T(8,128)(2,1)}, u32[]{:S(2)}, u32[]{:S(2)}) async-start(bf16[8,2,1,32,1024]{4,3,1,2,0:T(8,128)(2,1)} %bitcast.190), calls=%async_computation.4 | async-start | bytes 2097152 | tf_op jit(solution)/shard_map/all_to_all | solution.py:130
  435.5 17.2 %copy-start.35 = (f32[1024]{0:T(1024)S(1)}, f32[1024]{0:T(1024)}, u32[]{:S(2)}) copy-start(f32[1024]{0:T(1024)} %param.18) | copy-start | bytes 12292
  435.5 309.5 %reduce-scatter.9.cloned.1.call-start = ((), (), s32[]{:S(2)}) async-start(), calls=%async_computation.12 | async-start | bytes 10485760 | tf_op jit(solution)/shard_map/reduce_scatter | solution.py:191
  456.4 48.9 %collective-permute-start = (bf16[512,1024]{1,0:T(8,128)(2,1)S(1)}, bf16[512,1024]{1,0:T(8,128)(2,1)S(1)}, u32[]{:S(2)}, u32[]{:S(2)}) collective-permute-start(bf16[512,1024]{1,0:T(8,128)(2,1)S(1)} %get-tuple-element.75), channel_id=1, source_target_pairs={{0,1},{1,2},{2,3},{3,0},{4,5},{5,6},{6,7},{7,4},{8,9},{9,10},{10,1... | collective-permute-start | bytes 3145736 | tf_op jit(solution)/shard_map/ppermute | solution.py:179
  506.3 46.3 %collective-permute-start.1 = (bf16[512,1024]{1,0:T(8,128)(2,1)S(1)}, bf16[512,1024]{1,0:T(8,128)(2,1)}, u32[]{:S(2)}, u32[]{:S(2)}) collective-permute-start(bf16[512,1024]{1,0:T(8,128)(2,1)S(1)} %collective-permute-done), channel_id=1, source_target_pairs={{0,1},{1,2},{2,3},{3,0},{4,5},{5,6},{6,7},{7,4},{8,9},{9,10},{10,1... | collective-permute-start | bytes 3145736 | tf_op jit(solution)/shard_map/ppermute | solution.py:179
  552.5 24.8 %collective-permute-start.2 = (bf16[512,1024]{1,0:T(8,128)(2,1)}, bf16[512,1024]{1,0:T(8,128)(2,1)}, u32[]{:S(2)}, u32[]{:S(2)}) collective-permute-start(bf16[512,1024]{1,0:T(8,128)(2,1)} %collective-permute-done.1), channel_id=1, source_target_pairs={{0,1},{1,2},{2,3},{3,0},{4,5},{5,6},{6,7},{7,4},{8,9},{9,10},{10,1... | collective-permute-start | bytes 3145736 | tf_op jit(solution)/shard_map/ppermute | solution.py:179
  552.5 27.1 %copy-start.21 = (bf16[1024,1,1024]{2,1,0:T(2,128)(2,1)S(1)}, bf16[1024,1,1024]{2,1,0:T(2,128)(2,1)}, u32[]{:S(2)}) copy-start(bf16[1024,1,1024]{2,1,0:T(2,128)(2,1)} %get-tuple-element.63) | copy-start | bytes 6291460
  579.6 14.6 %copy-start.19 = (bf16[1024,1,1024]{2,1,0:T(2,128)(2,1)S(1)}, bf16[1024,1,1024]{2,1,0:T(2,128)(2,1)}, u32[]{:S(2)}) copy-start(bf16[1024,1,1024]{2,1,0:T(2,128)(2,1)} %get-tuple-element.62) | copy-start | bytes 6291460
  601.1 232.7 %all-gather.8.cloned.1.call-start = ((), (), s32[]{:S(2)}) async-start(), calls=%async_computation.13 | async-start | bytes 5242880 | tf_op jit(solution)/shard_map/all_gather | solution.py:200
  752.2 222.9 %reduce-scatter.11.cloned.1.call-start = ((), (), s32[]{:S(2)}) async-start(), calls=%async_computation.14 | async-start | bytes 5242880 | tf_op jit(solution)/shard_map/reduce_scatter | solution.py:233
  899.7 195.9 %all-reduce.4.cloned.1.call-start = ((), (), s32[]{:S(2)}) async-start(), calls=%async_computation.15 | async-start | bytes 12582912 | tf_op jit(solution)/shard_map/psum | solution.py:273
  929.0 46.1 %copy-start.30 = (f32[1024]{0:T(1024)S(1)}, f32[1024]{0:T(1024)}, u32[]{:S(2)}) copy-start(f32[1024]{0:T(1024)} %param.16) | copy-start | bytes 12292
  929.0 46.1 %copy-start.32 = (f32[512]{0:T(512)S(1)}, f32[512]{0:T(512)}, u32[]{:S(2)}) copy-start(f32[512]{0:T(512)} %copy-done.31) | copy-start | bytes 6148
  931.3 50.3 %all-to-all-start.1 = ((bf16[1,2,8,32,1024]{4,3,1,0,2:T(8,128)(2,1)}), bf16[1,2,8,32,1024]{4,3,1,0,2:T(8,128)(2,1)}, u32[]{:S(2)}, u32[]{:S(2)}) async-start(bf16[1,2,8,32,1024]{4,3,1,0,2:T(8,128)(2,1)} %copy.163), calls=%async_computation.3 | async-start | bytes 2097152 | tf_op jit(solution)/shard_map/all_to_all | solution.py:248
  981.6 168.7 %all-to-all-start.3 = ((bf16[1,2,8,32,1024]{4,3,1,0,2:T(8,128)(2,1)}), bf16[1,2,8,32,1024]{4,3,1,0,2:T(8,128)(2,1)}, u32[]{:S(2)}, u32[]{:S(2)}) async-start(bf16[1,2,8,32,1024]{4,3,1,0,2:T(8,128)(2,1)} %copy.182), calls=%async_computation.7 | async-start | bytes 2097152 | tf_op jit(solution)/shard_map/all_to_all | solution.py:255
  (32 other events, 120.4 us)
Sparse Core Ops, SparseCore 0:
  53.3 80.1 all-gather.3
  181.9 143.0 reduce-scatter.4
  328.7 81.4 all-gather.5
  431.4 100.3 reduce-scatter.6
  601.2 143.7 reduce-scatter.8
  752.3 81.4 all-gather.7
  899.8 75.2 reduce-scatter.10
  979.2 116.2 all-reduce.3
